TPU v7x, 128 devices: a whole 4x4x4 slice. The times are simulated.
128 devices in a mesh: row: 8 (over z, x_hi), col: 16 (over y, x_lo, core).
Axes of the slice: x: 4 (x_hi: 2, x_lo: 2; x = x_hi * 2 + x_lo), y: 4, z: 4, core: 2. Of those that a mesh axis runs over, the one named last changes fastest.
Arguments:
- pair: bfloat16 [1024, 1024, 128], P('row', 'col'), may hold values from -6 to 6
- grad_x: bfloat16 [1024, 1024, 64], P('row', 'col'), may hold values from -0.19921875 to 0.19921875
- norm_gain: float32 [128], replicated, may hold values from 0.1 to 1.9
- norm_bias: float32 [128], replicated, may hold values from -3 to 3
- proj_weight: bfloat16 [128, 256], replicated, may hold values from -0.5 to 0.5
- tile_mask: int32 [8, 8], replicated, may hold values 0 or 1
Outputs:
- grad_pair: bfloat16 [1024, 1024, 128], P('row', 'col')
All inputs are finite; a program needn't handle non-finite values.
Results may differ from a plain program's by a relative error of at most 0.012.
Values may be sent and summed in bfloat16 or wider, within the bound.
A program may use at most 128 MiB of HBM per device.

v0:
```python
import jax
import jax.numpy as jnp
from jax import lax
from jax.sharding import PartitionSpec as P

BLK = 128


def normalize(pair, norm_gain, norm_bias):
    values = pair.astype(jnp.float32)
    centred = values - jnp.mean(values, axis=-1, keepdims=True)
    variance = jnp.mean(centred * centred, axis=-1, keepdims=True)
    inverse = lax.rsqrt(variance + 1e-05)
    scaled = centred * inverse
    normed = (scaled * norm_gain + norm_bias).astype(jnp.bfloat16)
    return (scaled, inverse, normed)


def block_onehot(first_index, length, blocks):
    positions = first_index + jnp.arange(length, dtype=jnp.int32)
    block_range = jnp.arange(blocks, dtype=jnp.int32)
    return ((positions // BLK)[:, None] == block_range[None, :]).astype(jnp.float32)


def shards(pair, grad_x, norm_gain, norm_bias, proj_weight, tile_mask):
    row_count = pair.shape[0]
    col_count = pair.shape[1]
    hidden = grad_x.shape[2]
    total_rows = row_count * lax.axis_size("row")
    row_first = lax.axis_index("row") * row_count
    col_first = lax.axis_index("col") * col_count
    scaled, inverse, normed = normalize(pair, norm_gain, norm_bias)
    projected = jnp.einsum("ijc,cd->ijd", normed, proj_weight, preferred_element_type=jnp.float32)
    blocks = total_rows // BLK
    row_onehot = block_onehot(row_first, row_count, blocks)
    col_onehot = block_onehot(col_first, col_count, blocks)
    valid_tile = jnp.dot(jnp.dot(row_onehot, tile_mask.astype(jnp.float32)), col_onehot.T)[
        :, :, None
    ]
    lin_left = projected[:, :, 0:hidden]
    gate_left = projected[:, :, hidden : 2 * hidden]
    lin_right = projected[:, :, 2 * hidden : 3 * hidden]
    gate_right = projected[:, :, 3 * hidden : 4 * hidden]
    sig_left = jax.nn.sigmoid(gate_left)
    sig_right = jax.nn.sigmoid(gate_right)
    left_act = (valid_tile * sig_left * lin_left).astype(jnp.bfloat16)
    right_act = (valid_tile * sig_right * lin_right).astype(jnp.bfloat16)
    right_panel = lax.all_gather(right_act, "row", axis=0, tiled=True)
    grad_panel = lax.all_gather(grad_x, "col", axis=1, tiled=True)
    grad_left = jnp.einsum(
        "ijc,jkc->ikc", grad_panel, right_panel, preferred_element_type=jnp.float32
    )
    grad_right = lax.psum_scatter(
        jnp.einsum("ijc,ikc->jkc", grad_panel, left_act, preferred_element_type=jnp.float32).astype(
            jnp.bfloat16
        ),
        "row",
        scatter_dimension=0,
        tiled=True,
    ).astype(jnp.float32)
    grad_proj = jnp.concatenate(
        [
            grad_left * valid_tile * sig_left,
            grad_left * valid_tile * lin_left * sig_left * (1.0 - sig_left),
            grad_right * valid_tile * sig_right,
            grad_right * valid_tile * lin_right * sig_right * (1.0 - sig_right),
        ],
        axis=-1,
    ).astype(jnp.bfloat16)
    grad_normed = jnp.einsum(
        "ijd,cd->ijc", grad_proj, proj_weight, preferred_element_type=jnp.float32
    )
    scaled_grad = grad_normed * norm_gain
    result = inverse * (
        scaled_grad
        - jnp.mean(scaled_grad, axis=-1, keepdims=True)
        - scaled * jnp.mean(scaled_grad * scaled, axis=-1, keepdims=True)
    )
    return result.astype(jnp.bfloat16)


def solution(mesh):
    placed = (P("row", "col", None), P("row", "col", None), P(), P(), P(), P())
    return jax.shard_map(
        shards, mesh=mesh, in_specs=placed, out_specs=P("row", "col", None), check_vma=False
    )
```

profile of v0, /device:TPU:0, one launch (start us, length us, event | category | flops | bytes accessed | tf_op | source)
XLA Modules:
  0.0 447.1 jit_solution(17869223321097764401)
XLA Ops:
  6.6 3.3 copy.28
  10.0 0.5 convert_reduce_fusion
  10.5 0.8 fusion.13
  11.3 0.3 fusion.34
  11.7 1.4 fusion.22
  13.0 3.2 copy-done.1
  16.3 1.6 multiply_convert_fusion.5
  17.9 0.0 all-gather.3.cloned.1.call-update
  17.9 0.0 all-gather.5.cloned.1.call-start
  18.0 1.6 copy.32
  19.6 0.2 reduce-scatter.4.cloned.1.call-start
  19.9 113.4 %all-gather.3.cloned.1.call-done = bf16[1024,64,64]{0,2,1:T(8,128)(2,1)} async-done(((bf16[128,64,64]{0,2,1:T(8,128)(2,1)}), bf16[1024,64,64]{0,2,1:T(8,128)(2,1)}) %all-gather.3.cloned.1.call-update) | async-done | bytes 8388624 | tf_op jit(solution)/shard_map/all_gather | solution.py:48
  133.2 91.0 %all-gather.5.cloned.1.call-done = bf16[128,1024,64]{0,1,2:T(8,128)(2,1)} async-done(((bf16[128,64,64]{0,1,2:T(8,128)(2,1)}), bf16[128,1024,64]{0,1,2:T(8,128)(2,1)}) %all-gather.5.cloned.1.call-update) | async-done | bytes 16777232 | tf_op jit(solution)/shard_map/all_gather | solution.py:49
  224.2 18.1 %fusion = f32[64,64,128]{2,1,0:T(8,128)S(1)} fusion(bf16[128,1024,64]{0,1,2:T(8,128)(2,1)} %all-gather.5.cloned.1.call-done, bf16[1024,64,64]{0,2,1:T(8,128)(2,1)} %all-gather.3.cloned.1.call-done), kind=kOutput, calls=%fused_computation | convolution fusion | flops 1073741824 | bytes 27262976 | tf_op jit(solution)/shard_map/ijc,jkc->ikc/dot_general | solution.py:50
  242.3 5.7 %multiply_convert_fusion.4 = (bf16[128,64,64]{0,2,1:T(8,128)(2,1)}, bf16[128,64,64]{0,2,1:T(8,128)(2,1)}, bf16[128,64,64]{0,2,1:T(8,128)(2,1)S(1)}) fusion(f32[64,64,128]{2,1,0:T(8,128)S(1)} %fusion, f32[128,64]{0,1:T(8,128)S(1)} %fusion.34, f32[128,64,256]{0,2,1:T(8,128)} %copy-done.1), kind=kLoop, calls=%fused_computation.41 | loop fusion | flops 7340032 | bytes 9469952 | tf_op jit(solution)/shard_map/convert
  248.0 11.6 %convert_bitcast_fusion = bf16[1024,64,64]{0,1,2:T(8,128)(2,1)} fusion(bf16[128,1024,64]{0,1,2:T(8,128)(2,1)} %all-gather.5.cloned.1.call-done, bf16[128,64,64]{0,2,1:T(8,128)(2,1)S(1)} %get-tuple-element.11), kind=kOutput, calls=%fused_computation.2 | convolution fusion | flops 1077936128 | bytes 26214400 | tf_op jit(solution)/shard_map/ijc,ikc->jkc/dot_general | solution.py:54
  259.6 29.2 %copy.44 = bf16[1024,64,64]{2,1,0:T(8,128)(2,1)} copy(bf16[1024,64,64]{0,1,2:T(8,128)(2,1)} %convert_bitcast_fusion) | data formatting | bytes 16777216
  288.8 22.6 %reshape.62 = bf16[1024,4096]{1,0:T(8,128)(2,1)} reshape(bf16[1024,64,64]{2,1,0:T(8,128)(2,1)} %copy.44) | data formatting | bytes 16777216
  311.3 115.8 %reduce-scatter.4.cloned.1.call-done = bf16[128,4096]{1,0:T(8,128)(2,1)} async-done(((bf16[1024,4096]{1,0:T(8,128)(2,1)}), bf16[128,4096]{1,0:T(8,128)(2,1)}) %reduce-scatter.4.cloned.1.call-update) | async-done | bytes 1048592
  427.2 1.6 copy.47
  428.8 3.3 multiply_convert_fusion.1
  432.1 1.5 multiply_reduce_fusion
  433.7 2.8 fusion.12
  436.5 4.1 copy.40
  (23 shorter events, 0.1 us)
Async XLA Ops:
  6.5 5.1 %copy-start = (bf16[128,256]{1,0:T(8,128)(2,1)S(1)}, bf16[128,256]{1,0:T(8,128)(2,1)}, u32[]{:S(2)}) copy-start(bf16[128,256]{1,0:T(8,128)(2,1)} %param.10) | copy-start | bytes 196612
  6.5 126.7 %all-gather.3.cloned.1.call-start = ((), (), s32[]{:S(2)}) async-start(), calls=%async_computation.1 | async-start | bytes 9437184 | tf_op jit(solution)/shard_map/all_gather | solution.py:48
  6.6 4.7 %copy-start.7 = (s32[8,8]{1,0:T(8,128)S(1)}, s32[8,8]{1,0:T(8,128)}, u32[]{:S(2)}) copy-start(s32[8,8]{1,0:T(8,128)} %param.11) | copy-start | bytes 772
  6.6 5.1 %copy-start.5 = (f32[128]{0:T(128)S(1)}, f32[128]{0:T(128)}, u32[]{:S(2)}) copy-start(f32[128]{0:T(128)} %param.8) | copy-start | bytes 1540
  6.6 5.1 %copy-start.6 = (f32[128]{0:T(128)S(1)}, f32[128]{0:T(128)}, u32[]{:S(2)}) copy-start(f32[128]{0:T(128)} %param.9) | copy-start | bytes 1540
  13.0 3.2 copy-start.1
  16.3 1.7 copy-start.4
  17.9 206.3 %all-gather.5.cloned.1.call-start = ((), (), s32[]{:S(2)}) async-start(), calls=%async_computation.2 | async-start | bytes 17825792 | tf_op jit(solution)/shard_map/all_gather | solution.py:49
  19.6 407.5 %reduce-scatter.4.cloned.1.call-start = ((), (), s32[]{:S(2)}) async-start(), calls=%async_computation.3 | async-start | bytes 9437184
  428.8 3.3 copy-start.2
  428.8 3.3 copy-start.3
Sparse Core Ops, SparseCore 0:
  18.0 115.1 all-gather.2
  134.9 89.2 all-gather.4
  311.5 115.6 reduce-scatter.3
where the time goes:
time: 448 us; the launch traced here: 447 us
  waiting for transfers between devices  320 us (71%)
  local copies, waits for them, and re-layouts  65.7 us (15%)
  matrix products  32.9 us (7%)
  other arithmetic  14.7 us (3%)
  between operations  13.3 us (3%)
    unnamed x4, waiting for transfers between devices  116 us
    all_gather x1, waiting for transfers between devices, shards(): right_panel = lax.all_gather(right_act, 'row', axis=0, tiled=True)  113 us
    all_gather x1, waiting for transfers between devices, shards(): grad_panel = lax.all_gather(grad_x, 'col', axis=1, tiled=True)  91 us
    unnamed x21, local copies, waits for them, and re-layouts  61.6 us
    dot_general x1, matrix products, shards(): jnp.einsum('ijc,jkc->ikc', grad_panel, right_panel, preferred_element_typ...  18.1 us
    dot_general x1, matrix products, shards(): jnp.einsum('ijc,ikc->jkc', grad_panel, left_act, preferred_element_type=j...  11.6 us
    another operation x2, other arithmetic  8.98 us
  transfers between devices with their start and end apart: 3, of which 3 were waited for; matrix products, arithmetic and copies ran while one was open for 0% of the time, Pallas kernels for 0%

commit v1 on v0

v1 whole, which is shorter than its diff:
```python
import functools

import jax
import jax.numpy as jnp
from jax import lax
from jax.experimental import pallas as pl
from jax.experimental.pallas import tpu as pltpu
from jax.sharding import PartitionSpec as P

MESH = pl.DeviceIdType.MESH
F32 = jnp.float32
BF16 = jnp.bfloat16


def ring_distance(offset, size):
    return min(offset, size - offset)


def send_order(X, Y, Z):
    offsets = [(a, b, c) for a in range(X) for b in range(Y) for c in range(Z)]
    offsets.remove((0, 0, 0))
    state, shuffled = 12345, []
    while offsets:
        state = (state * 1103515245 + 12345) % (1 << 31)
        shuffled.append(offsets.pop((state >> 8) % len(offsets)))
    paired, seen = [], set()
    for offset in shuffled:
        for one in (offset, ((-offset[0]) % X, (-offset[1]) % Y, (-offset[2]) % Z)):
            if one not in seen:
                seen.add(one)
                paired.append(one)
    def far(o):
        return ring_distance(o[0], X) + ring_distance(o[1], Y) + ring_distance(o[2], Z)

    return sorted(paired, key=lambda o: -far(o))


def kernel(
    RN,
    QN,
    mask_ref,
    pair_hbm,
    grad_hbm,
    gain_ref,
    bias_ref,
    w_ref,
    out_hbm,
    pair_v,
    pair_f,
    grad_v,
    f1,
    f2,
    f3,
    gs,
    ls,
    rs,
    gt,
    lt,
    rt,
    ogr,
    ogl,
    rgr,
    rgl,
    act,
    scaled_s,
    inv_s,
    part,
    out_v,
    wt_s,
    gain_s,
    bias_s,
    load_sem,
    send_sem,
    recv_sem,
    out_sem,
):
    TI, TJ, C = pair_v.shape
    H = gs.shape[0]
    X, Y, Z = 4, QN // 4, RN // 2
    QP = QN // 2
    row, col = lax.axis_index("row"), lax.axis_index("col")
    z, xh = row // 2, row % 2
    qp, core = col // 2, col % 2
    y, xl = qp // 2, qp % 2
    x = xh * 2 + xl
    me = row * QP + qp

    grad_load = pltpu.make_async_copy(grad_hbm, grad_v, load_sem.at[0])
    pair_load = pltpu.make_async_copy(pair_hbm, pair_v, load_sem.at[1])
    grad_load.start()
    pair_load.start()

    peers = []
    for dx, dy, dz in send_order(X, Y, Z):
        px, py, pz = (x + dx) % X, (y + dy) % Y, (z + dz) % Z
        peers.append((pz * 2 + px // 2, py * 2 + px % 2))

    barrier = pltpu.get_barrier_semaphore()
    for prow, pqp in peers:
        pl.semaphore_signal(
            barrier, inc=1, device_id=(prow, pqp * 2 + core), device_id_type=MESH
        )
    pl.semaphore_signal(barrier, inc=1, device_id=(row, qp * 2 + 1 - core), device_id_type=MESH)

    gain_s[...] = jnp.transpose(jnp.broadcast_to(gain_ref[...], (C, C)))
    bias_s[...] = jnp.transpose(jnp.broadcast_to(bias_ref[...], (C, C)))
    wt_s[...] = jnp.transpose(w_ref[...].astype(F32)).astype(BF16)

    def scatter(n, src_of, dst, own_src):
        pltpu.make_async_copy(own_src, dst, recv_sem.at[n]).start()
        for prow, pqp in peers:
            pltpu.make_async_remote_copy(
                src_ref=src_of(prow, pqp),
                dst_ref=dst,
                send_sem=send_sem.at[n],
                recv_sem=recv_sem.at[n],
                device_id=(prow, pqp * 2 + core),
                device_id_type=MESH,
            ).start()

    def wait_for(ref, sem):
        pltpu.make_async_copy(ref, ref, sem).wait()

    grad_load.wait()

    @pl.loop(0, TJ)
    def _(j):
        f1[pl.ds(j * H, H), :] = grad_v[j].astype(F32)

    @pl.loop(0, H)
    def _(c):
        gs[c] = f1[pl.ds(c, TJ, stride=H), :].astype(BF16)

    pl.semaphore_wait(barrier, len(peers) + 1)
    lanes = pl.ds(pl.multiple_of(row * TI, TI), TI)
    by_channel = lambda ref: (lambda prow, pqp: ref.at[prow * QP + pqp])
    scatter(0, by_channel(gs), gt.at[qp, pl.ds(pl.multiple_of(core * TJ, TJ), TJ), lanes], gs.at[me])

    pair_load.wait()

    @pl.loop(0, TI)
    def _(i):
        pair_f[pl.ds(i * TJ, TJ), :] = pair_v[i].astype(F32)

    valid = mask_ref[row, col // 2].astype(F32)
    eye = (
        lax.broadcasted_iota(jnp.int32, (C, C), 0) == lax.broadcasted_iota(jnp.int32, (C, C), 1)
    ).astype(F32).astype(BF16)

    @pl.loop(0, TJ // 2)
    def _(m):
        tokens = jnp.concatenate(
            [pair_f[pl.ds(2 * m + s, TI, stride=TJ), :] for s in (0, 1)], axis=0
        ).astype(BF16)
        values = lax.dot_general(
            eye, tokens, (((1,), (1,)), ((), ())), preferred_element_type=F32
        )
        centred = values - jnp.mean(values, axis=0, keepdims=True)
        variance = jnp.mean(centred * centred, axis=0, keepdims=True)
        inverse = lax.rsqrt(variance + 1e-05)
        scaled = centred * inverse
        gain = jnp.concatenate([gain_s[...], gain_s[...]], axis=1)
        bias = jnp.concatenate([bias_s[...], bias_s[...]], axis=1)
        normed = (scaled * gain + bias).astype(BF16)
        scaled_s[m] = scaled
        inv_s[m] = jnp.broadcast_to(inverse, (8, 2 * TI))
        projected = jnp.dot(wt_s[...], normed, preferred_element_type=F32)
        for side, f in ((0, f2), (1, f3)):
            lin = projected[2 * side * H : (2 * side + 1) * H]
            sig = jax.nn.sigmoid(projected[(2 * side + 1) * H : (2 * side + 2) * H])
            gated = valid * sig
            act[m, pl.ds(2 * side * H, H)] = gated
            act[m, pl.ds((2 * side + 1) * H, H)] = lin * (1.0 - sig)
            activation = gated * lin
            for s in (0, 1):
                f[pl.ds(2 * m + s, H, stride=TJ), :] = activation[:, s * TI : (s + 1) * TI]

    here = (pl.ds(pl.multiple_of(qp * TJ, TJ), TJ), lanes)
    for n, f, s, t in ((1, f2, ls, lt), (2, f3, rs, rt)):

        @pl.loop(0, H)
        def _(c):
            s[c] = f[pl.ds(c * TJ, TJ), :].astype(BF16)

        scatter(n, by_channel(s), t.at[here], s.at[me])

    half = gt.at[:, pl.ds(pl.multiple_of(core * TJ, TJ), TJ), :]
    other = gt.at[:, pl.ds(pl.multiple_of((1 - core) * TJ, TJ), TJ), :]
    wait_for(half, recv_sem.at[0])
    share = pltpu.make_async_remote_copy(
        src_ref=half,
        dst_ref=half,
        send_sem=send_sem.at[5],
        recv_sem=recv_sem.at[5],
        device_id=(row, qp * 2 + 1 - core),
        device_id_type=MESH,
    )
    share.start()
    wait_for(other, recv_sem.at[5])

    def block_of(ref):
        return lambda prow, pqp: ref.at[
            pl.ds(pl.multiple_of(pqp * TJ, TJ), TJ), pl.ds(pl.multiple_of(prow * TI, TI), TI)
        ]

    wait_for(lt, recv_sem.at[1])

    @pl.loop(0, RN // 2)
    def _(n):
        g = gt[pl.ds(n * 2, 2)].reshape(2 * TI, RN * TI)
        ogr[:, pl.ds(pl.multiple_of(n * 2 * TI, 2 * TI), 2 * TI)] = lax.dot_general(
            lt[...], g, (((1,), (1,)), ((), ())), preferred_element_type=F32
        ).astype(BF16)

    scatter(3, block_of(ogr), rgr.at[me], block_of(ogr)(row, qp))

    wait_for(rt, recv_sem.at[2])

    @pl.loop(0, RN // 2)
    def _(n):
        cols = pl.ds(pl.multiple_of(n * 2 * TI, 2 * TI), 2 * TI)
        g = gt[:, :, cols].reshape(RN * TI, 2 * TI)
        ogl[:, cols] = jnp.dot(rt[...], g, preferred_element_type=F32).astype(BF16)

    scatter(4, block_of(ogl), rgl.at[me], block_of(ogl)(row, qp))

    def grad_proj(f, m, side):
        g = jnp.concatenate([f[pl.ds(2 * m + s, H, stride=TJ), :] for s in (0, 1)], axis=1)
        lin = g * act[m, pl.ds(2 * side * H, H)]
        gate = lin * act[m, pl.ds((2 * side + 1) * H, H)]
        return jnp.concatenate([lin, gate], axis=0).astype(BF16)

    wait_for(rgr, recv_sem.at[3])

    @pl.loop(0, H)
    def _(c):
        f3[pl.ds(c * TJ, TJ), :] = rgr[c].astype(F32)

    @pl.loop(0, TJ // 2)
    def _(m):
        part[m] = jnp.dot(
            w_ref[:, 2 * H : 4 * H], grad_proj(f3, m, 1), preferred_element_type=F32
        )

    wait_for(rgl, recv_sem.at[4])

    @pl.loop(0, H)
    def _(c):
        f2[pl.ds(c * TJ, TJ), :] = rgl[c].astype(F32)

    @pl.loop(0, TJ // 2)
    def _(m):
        grad_normed = part[m] + jnp.dot(
            w_ref[:, 0 : 2 * H], grad_proj(f2, m, 0), preferred_element_type=F32
        )
        gain = jnp.concatenate([gain_s[...], gain_s[...]], axis=1)
        scaled = scaled_s[m]
        g = grad_normed * gain
        result = inv_s[m, 0:1] * (
            g
            - jnp.mean(g, axis=0, keepdims=True)
            - scaled * jnp.mean(g * scaled, axis=0, keepdims=True)
        )
        result = result.astype(BF16)
        for s in (0, 1):
            out_v[2 * m + s] = result[:, s * TI : (s + 1) * TI]

    store = pltpu.make_async_copy(out_v, out_hbm, out_sem)
    store.start()

    for n, buf in enumerate((gs, ls, rs, rgr, rgl)):
        if len(peers):
            wait_for(buf.at[pl.ds(0, len(peers))], send_sem.at[n])
    wait_for(half, send_sem.at[5])
    store.wait()


def shards(RN, QN, pair, grad_x, norm_gain, norm_bias, proj_weight, tile_mask):
    TI, TJ, C = pair.shape
    H = grad_x.shape[2]
    QP = QN // 2
    N = RN * TI
    vmem = lambda *shape: pltpu.VMEM(shape[:-1], shape[-1])
    any_space = pl.BlockSpec(memory_space=pl.ANY)
    in_vmem = pl.BlockSpec(memory_space=pltpu.VMEM)
    out = pl.pallas_call(
        functools.partial(kernel, RN, QN),
        out_shape=jax.ShapeDtypeStruct((TJ, C, TI), BF16),
        in_specs=[
            pl.BlockSpec(memory_space=pltpu.SMEM),
            any_space,
            any_space,
            in_vmem,
            in_vmem,
            in_vmem,
        ],
        out_specs=any_space,
        scratch_shapes=[
            vmem(TI, TJ, C, BF16),
            vmem(TI * TJ, C, F32),
            vmem(TJ, H, TI, BF16),
            vmem(TJ * H, TI, F32),
            vmem(TJ * H, TI, F32),
            vmem(TJ * H, TI, F32),
            vmem(H, TJ, TI, BF16),
            vmem(H, TJ, TI, BF16),
            vmem(H, TJ, TI, BF16),
            vmem(QP, 2 * TJ, N, BF16),
            vmem(QP * TJ, N, BF16),
            vmem(QP * TJ, N, BF16),
            vmem(QP * TJ, N, BF16),
            vmem(QP * TJ, N, BF16),
            vmem(H, TJ, TI, BF16),
            vmem(H, TJ, TI, BF16),
            vmem(TJ // 2, 4 * H, 2 * TI, F32),
            vmem(TJ // 2, C, 2 * TI, F32),
            vmem(TJ // 2, 8, 2 * TI, F32),
            vmem(TJ // 2, C, 2 * TI, F32),
            vmem(TJ, C, TI, BF16),
            vmem(4 * H, C, BF16),
            vmem(C, C, F32),
            vmem(C, C, F32),
            pltpu.SemaphoreType.DMA((2,)),
            pltpu.SemaphoreType.DMA((6,)),
            pltpu.SemaphoreType.DMA((6,)),
            pltpu.SemaphoreType.DMA(()),
        ],
        compiler_params=pltpu.CompilerParams(
            collective_id=0, has_side_effects=True, vmem_limit_bytes=60 << 20
        ),
    )(
        tile_mask,
        pair,
        jnp.transpose(grad_x, (1, 2, 0)),
        norm_gain.reshape(1, C),
        norm_bias.reshape(1, C),
        proj_weight,
    )
    return jnp.transpose(out, (2, 0, 1))


def solution(mesh):
    placed = (P("row", "col", None), P("row", "col", None), P(), P(), P(), P())
    body = functools.partial(shards, mesh.shape["row"], mesh.shape["col"])
    return jax.shard_map(
        body, mesh=mesh, in_specs=placed, out_specs=P("row", "col", None), check_vma=False
    )
```

time: 448 us -> 95.3 us (0.21)
  the two profiles are of different devices: /device:TPU:0 before, /device:TPU:4 now
where the time goes in v1:
time: 95.3 us; the launch traced here: 95 us
  Pallas kernels  90.9 us (95%)
  local copies, waits for them, and re-layouts  4.12 us (4%)
    pallas_call x1, Pallas kernels, shards(): pl.pallas_call(functools.partial(kernel, RN, QN), out_shape=jax.ShapeDtyp...  90.9 us
    transpose x1, local copies, waits for them, and re-layouts, shards(): return jnp.transpose(out, (2, 0, 1))  4.12 us

profile of v1, /device:TPU:4, one launch (start us, length us, event | category | flops | bytes accessed | tf_op | source)
XLA Modules:
  0.0 95.0 jit_solution(10942808391024922476)
XLA Ops:
  0.0 90.9 %shard_map.64 = bf16[64,128,128]{2,1,0:T(8,128)(2,1)} custom-call(s32[8,8]{1,0:T(8,128)} %mask_ref.1, bf16[128,64,128]{2,1,0:T(8,128)(2,1)} %pair_hbm.1, bf16[64,64,128]{2,1,0:T(8,128)(2,1)} %bitcast.5, f32[1,128]{1,0:T(1,128)} %bitcast.6, f32[1,128]{1,0:T(1,128)} %bitcast.7, bf16[128,256]{1,0:T(8,128)(2,1)} %w_ref.1), custom_call_target="tpu_custom_call" | custom-call | tf_op jit(solution)/shard_map/pallas_call | solution.py:286
  90.9 4.1 %copy.7 = bf16[128,64,128]{2,1,0:T(8,128)(2,1)} copy(bf16[128,64,128]{0,2,1:T(8,128)(2,1)} %bitcast.4) | data formatting | bytes 4194304 | tf_op jit(solution)/shard_map/transpose | solution.py:339

commit v2 on v1

--- a/solution.py
+++ b/solution.py
@@ -65,6 +65,7 @@
     scaled_s,
     inv_s,
     part,
+    normed_s,
     out_v,
     wt_s,
     gain_s,
@@ -78,6 +79,7 @@
     H = gs.shape[0]
     X, Y, Z = 4, QN // 4, RN // 2
     QP = QN // 2
+    pitch = f1.shape[0] // TJ
     row, col = lax.axis_index("row"), lax.axis_index("col")
     z, xh = row // 2, row % 2
     qp, core = col // 2, col % 2
@@ -123,13 +125,13 @@
 
     grad_load.wait()
 
-    @pl.loop(0, TJ)
+    @pl.loop(0, TJ, unroll=4)
     def _(j):
-        f1[pl.ds(j * H, H), :] = grad_v[j].astype(F32)
-
-    @pl.loop(0, H)
+        f1[pl.ds(j * pitch, H), :] = grad_v[j].astype(F32)
+
+    @pl.loop(0, H, unroll=4)
     def _(c):
-        gs[c] = f1[pl.ds(c, TJ, stride=H), :].astype(BF16)
+        gs[c] = f1[pl.ds(c, TJ, stride=pitch), :].astype(BF16)
 
     pl.semaphore_wait(barrier, len(peers) + 1)
     lanes = pl.ds(pl.multiple_of(row * TI, TI), TI)
@@ -138,19 +140,41 @@
 
     pair_load.wait()
 
-    @pl.loop(0, TI)
+    @pl.loop(0, TI, unroll=4)
     def _(i):
-        pair_f[pl.ds(i * TJ, TJ), :] = pair_v[i].astype(F32)
+        pair_f[pl.ds(i * pitch, TJ), :] = pair_v[i].astype(F32)
 
     valid = mask_ref[row, col // 2].astype(F32)
     eye = (
         lax.broadcasted_iota(jnp.int32, (C, C), 0) == lax.broadcasted_iota(jnp.int32, (C, C), 1)
     ).astype(F32).astype(BF16)
 
-    @pl.loop(0, TJ // 2)
+    def activate(m, normed, side, f):
+        projected = jnp.dot(
+            wt_s[pl.ds(2 * side * H, 2 * H), :], normed, preferred_element_type=F32
+        )
+        lin = projected[0:H]
+        sig = jax.nn.sigmoid(projected[H : 2 * H])
+        gated = valid * sig
+        act[m, pl.ds(2 * side * H, H)] = gated
+        act[m, pl.ds((2 * side + 1) * H, H)] = lin * (1.0 - sig)
+        activation = gated * lin
+        for s in (0, 1):
+            f[pl.ds(2 * m + s, H, stride=pitch), :] = activation[:, s * TI : (s + 1) * TI]
+
+    here = (pl.ds(pl.multiple_of(qp * TJ, TJ), TJ), lanes)
+
+    def send_activation(n, f, s, t):
+        @pl.loop(0, H, unroll=4)
+        def _(c):
+            s[c] = f[pl.ds(c * pitch, TJ), :].astype(BF16)
+
+        scatter(n, by_channel(s), t.at[here], s.at[me])
+
+    @pl.loop(0, TJ // 2, unroll=2)
     def _(m):
         tokens = jnp.concatenate(
-            [pair_f[pl.ds(2 * m + s, TI, stride=TJ), :] for s in (0, 1)], axis=0
+            [pair_f[pl.ds(2 * m + s, TI, stride=pitch), :] for s in (0, 1)], axis=0
         ).astype(BF16)
         values = lax.dot_general(
             eye, tokens, (((1,), (1,)), ((), ())), preferred_element_type=F32
@@ -164,25 +188,16 @@
         normed = (scaled * gain + bias).astype(BF16)
         scaled_s[m] = scaled
         inv_s[m] = jnp.broadcast_to(inverse, (8, 2 * TI))
-        projected = jnp.dot(wt_s[...], normed, preferred_element_type=F32)
-        for side, f in ((0, f2), (1, f3)):
-            lin = projected[2 * side * H : (2 * side + 1) * H]
-            sig = jax.nn.sigmoid(projected[(2 * side + 1) * H : (2 * side + 2) * H])
-            gated = valid * sig
-            act[m, pl.ds(2 * side * H, H)] = gated
-            act[m, pl.ds((2 * side + 1) * H, H)] = lin * (1.0 - sig)
-            activation = gated * lin
-            for s in (0, 1):
-                f[pl.ds(2 * m + s, H, stride=TJ), :] = activation[:, s * TI : (s + 1) * TI]
-
-    here = (pl.ds(pl.multiple_of(qp * TJ, TJ), TJ), lanes)
-    for n, f, s, t in ((1, f2, ls, lt), (2, f3, rs, rt)):
-
-        @pl.loop(0, H)
-        def _(c):
-            s[c] = f[pl.ds(c * TJ, TJ), :].astype(BF16)
-
-        scatter(n, by_channel(s), t.at[here], s.at[me])
+        normed_s[m] = normed
+        activate(m, normed, 0, f2)
+
+    send_activation(1, f2, ls, lt)
+
+    @pl.loop(0, TJ // 2, unroll=2)
+    def _(m):
+        activate(m, normed_s[m], 1, f3)
+
+    send_activation(2, f3, rs, rt)
 
     half = gt.at[:, pl.ds(pl.multiple_of(core * TJ, TJ), TJ), :]
     other = gt.at[:, pl.ds(pl.multiple_of((1 - core) * TJ, TJ), TJ), :]
@@ -190,13 +205,13 @@
     share = pltpu.make_async_remote_copy(
         src_ref=half,
         dst_ref=half,
-        send_sem=send_sem.at[5],
-        recv_sem=recv_sem.at[5],
+        send_sem=send_sem.at[6],
+        recv_sem=recv_sem.at[6],
         device_id=(row, qp * 2 + 1 - core),
         device_id_type=MESH,
     )
     share.start()
-    wait_for(other, recv_sem.at[5])
+    wait_for(other, recv_sem.at[6])
 
     def block_of(ref):
         return lambda prow, pqp: ref.at[
@@ -222,57 +237,69 @@
         g = gt[:, :, cols].reshape(RN * TI, 2 * TI)
         ogl[:, cols] = jnp.dot(rt[...], g, preferred_element_type=F32).astype(BF16)
 
-    scatter(4, block_of(ogl), rgl.at[me], block_of(ogl)(row, qp))
+    HK = TJ // 2
+
+    def part_of(ref, half_k):
+        return lambda prow, pqp: ref.at[
+            pl.ds(pl.multiple_of(pqp * TJ + half_k * HK, HK), HK),
+            pl.ds(pl.multiple_of(prow * TI, TI), TI),
+        ]
+
+    for hk in (0, 1):
+        scatter(4 + hk, part_of(ogl, hk), rgl.at[me, pl.ds(hk * HK, HK)], part_of(ogl, hk)(row, qp))
 
     def grad_proj(f, m, side):
-        g = jnp.concatenate([f[pl.ds(2 * m + s, H, stride=TJ), :] for s in (0, 1)], axis=1)
+        g = jnp.concatenate([f[pl.ds(2 * m + s, H, stride=pitch), :] for s in (0, 1)], axis=1)
         lin = g * act[m, pl.ds(2 * side * H, H)]
         gate = lin * act[m, pl.ds((2 * side + 1) * H, H)]
         return jnp.concatenate([lin, gate], axis=0).astype(BF16)
 
     wait_for(rgr, recv_sem.at[3])
 
-    @pl.loop(0, H)
+    @pl.loop(0, H, unroll=4)
     def _(c):
-        f3[pl.ds(c * TJ, TJ), :] = rgr[c].astype(F32)
-
-    @pl.loop(0, TJ // 2)
+        f3[pl.ds(c * pitch, TJ), :] = rgr[c].astype(F32)
+
+    @pl.loop(0, TJ // 2, unroll=2)
     def _(m):
         part[m] = jnp.dot(
             w_ref[:, 2 * H : 4 * H], grad_proj(f3, m, 1), preferred_element_type=F32
         )
 
-    wait_for(rgl, recv_sem.at[4])
-
-    @pl.loop(0, H)
-    def _(c):
-        f2[pl.ds(c * TJ, TJ), :] = rgl[c].astype(F32)
-
-    @pl.loop(0, TJ // 2)
-    def _(m):
-        grad_normed = part[m] + jnp.dot(
-            w_ref[:, 0 : 2 * H], grad_proj(f2, m, 0), preferred_element_type=F32
-        )
-        gain = jnp.concatenate([gain_s[...], gain_s[...]], axis=1)
-        scaled = scaled_s[m]
-        g = grad_normed * gain
-        result = inv_s[m, 0:1] * (
-            g
-            - jnp.mean(g, axis=0, keepdims=True)
-            - scaled * jnp.mean(g * scaled, axis=0, keepdims=True)
-        )
-        result = result.astype(BF16)
-        for s in (0, 1):
-            out_v[2 * m + s] = result[:, s * TI : (s + 1) * TI]
-
-    store = pltpu.make_async_copy(out_v, out_hbm, out_sem)
-    store.start()
-
-    for n, buf in enumerate((gs, ls, rs, rgr, rgl)):
-        if len(peers):
-            wait_for(buf.at[pl.ds(0, len(peers))], send_sem.at[n])
-    wait_for(half, send_sem.at[5])
-    store.wait()
+    for hk in (0, 1):
+        wait_for(rgl.at[:, pl.ds(hk * HK, HK)], recv_sem.at[4 + hk])
+
+        @pl.loop(0, H, unroll=4)
+        def _(c):
+            f2[pl.ds(c * pitch + hk * HK, HK), :] = rgl[c, pl.ds(hk * HK, HK)].astype(F32)
+
+        @pl.loop(hk * HK // 2, (hk + 1) * HK // 2, unroll=2)
+        def _(m):
+            grad_normed = part[m] + jnp.dot(
+                w_ref[:, 0 : 2 * H], grad_proj(f2, m, 0), preferred_element_type=F32
+            )
+            gain = jnp.concatenate([gain_s[...], gain_s[...]], axis=1)
+            scaled = scaled_s[m]
+            g = grad_normed * gain
+            result = inv_s[m, 0:1] * (
+                g
+                - jnp.mean(g, axis=0, keepdims=True)
+                - scaled * jnp.mean(g * scaled, axis=0, keepdims=True)
+            )
+            result = result.astype(BF16)
+            for s in (0, 1):
+                out_v[2 * m + s] = result[:, s * TI : (s + 1) * TI]
+
+        rows = pl.ds(hk * HK, HK)
+        pltpu.make_async_copy(out_v.at[rows], out_hbm.at[rows], out_sem.at[hk]).start()
+
+    for n, buf in enumerate((gs, ls, rs, rgr)):
+        wait_for(buf.at[pl.ds(0, len(peers))], send_sem.at[n])
+    for hk in (0, 1):
+        rows = pl.ds(hk * HK, HK)
+        wait_for(rgl.at[pl.ds(0, len(peers)), rows], send_sem.at[4 + hk])
+        pltpu.make_async_copy(out_v.at[rows], out_hbm.at[rows], out_sem.at[hk]).wait()
+    wait_for(half, send_sem.at[6])
 
 
 def shards(RN, QN, pair, grad_x, norm_gain, norm_bias, proj_weight, tile_mask):
@@ -280,6 +307,7 @@
     H = grad_x.shape[2]
     QP = QN // 2
     N = RN * TI
+    pitch = TJ + 8
     vmem = lambda *shape: pltpu.VMEM(shape[:-1], shape[-1])
     any_space = pl.BlockSpec(memory_space=pl.ANY)
     in_vmem = pl.BlockSpec(memory_space=pltpu.VMEM)
@@ -297,11 +325,11 @@
         out_specs=any_space,
         scratch_shapes=[
             vmem(TI, TJ, C, BF16),
-            vmem(TI * TJ, C, F32),
+            vmem(TI * pitch, C, F32),
             vmem(TJ, H, TI, BF16),
-            vmem(TJ * H, TI, F32),
-            vmem(TJ * H, TI, F32),
-            vmem(TJ * H, TI, F32),
+            vmem(TJ * pitch, TI, F32),
+            vmem(TJ * pitch, TI, F32),
+            vmem(TJ * pitch, TI, F32),
             vmem(H, TJ, TI, BF16),
             vmem(H, TJ, TI, BF16),
             vmem(H, TJ, TI, BF16),
@@ -316,14 +344,15 @@
             vmem(TJ // 2, C, 2 * TI, F32),
             vmem(TJ // 2, 8, 2 * TI, F32),
             vmem(TJ // 2, C, 2 * TI, F32),
+            vmem(TJ // 2, C, 2 * TI, BF16),
             vmem(TJ, C, TI, BF16),
             vmem(4 * H, C, BF16),
             vmem(C, C, F32),
             vmem(C, C, F32),
             pltpu.SemaphoreType.DMA((2,)),
-            pltpu.SemaphoreType.DMA((6,)),
-            pltpu.SemaphoreType.DMA((6,)),
-            pltpu.SemaphoreType.DMA(()),
+            pltpu.SemaphoreType.DMA((7,)),
+            pltpu.SemaphoreType.DMA((7,)),
+            pltpu.SemaphoreType.DMA((2,)),
         ],
         compiler_params=pltpu.CompilerParams(
             collective_id=0, has_side_effects=True, vmem_limit_bytes=60 << 20

time: 95.3 us -> 79.2 us (0.83)
  the two profiles are of different devices: /device:TPU:4 before, /device:TPU:0 now
where the time goes in v2:
time: 79.2 us; the launch traced here: 78.8 us
  Pallas kernels  74.6 us (94%)
  local copies, waits for them, and re-layouts  4.12 us (5%)
    pallas_call x1, Pallas kernels, shards(): pl.pallas_call(functools.partial(kernel, RN, QN), out_shape=jax.ShapeDtyp...  74.6 us
    transpose x1, local copies, waits for them, and re-layouts, shards(): return jnp.transpose(out, (2, 0, 1))  4.12 us

profile of v2, /device:TPU:0, one launch (start us, length us, event | category | flops | bytes accessed | tf_op | source)
XLA Modules:
  0.0 78.8 jit_solution(12467234209832891996)
XLA Ops:
  0.0 74.6 %shard_map.64 = bf16[64,128,128]{2,1,0:T(8,128)(2,1)} custom-call(s32[8,8]{1,0:T(8,128)} %mask_ref.1, bf16[128,64,128]{2,1,0:T(8,128)(2,1)} %pair_hbm.1, bf16[64,64,128]{2,1,0:T(8,128)(2,1)} %bitcast.5, f32[1,128]{1,0:T(1,128)} %bitcast.6, f32[1,128]{1,0:T(1,128)} %bitcast.7, bf16[128,256]{1,0:T(8,128)(2,1)} %w_ref.1), custom_call_target="tpu_custom_call" | custom-call | tf_op jit(solution)/shard_map/pallas_call | solution.py:314
  74.6 4.1 %copy.7 = bf16[128,64,128]{2,1,0:T(8,128)(2,1)} copy(bf16[128,64,128]{0,2,1:T(8,128)(2,1)} %bitcast.4) | data formatting | bytes 4194304 | tf_op jit(solution)/shard_map/transpose | solution.py:368

commit v3 on v2

--- a/solution.py
+++ b/solution.py
@@ -44,7 +44,7 @@
     gain_ref,
     bias_ref,
     w_ref,
-    out_hbm,
+    out_ref,
     pair_v,
     pair_f,
     grad_v,
@@ -66,14 +66,12 @@
     inv_s,
     part,
     normed_s,
-    out_v,
     wt_s,
     gain_s,
     bias_s,
     load_sem,
     send_sem,
     recv_sem,
-    out_sem,
 ):
     TI, TJ, C = pair_v.shape
     H = gs.shape[0]
@@ -286,19 +284,20 @@
                 - jnp.mean(g, axis=0, keepdims=True)
                 - scaled * jnp.mean(g * scaled, axis=0, keepdims=True)
             )
-            result = result.astype(BF16)
             for s in (0, 1):
-                out_v[2 * m + s] = result[:, s * TI : (s + 1) * TI]
-
-        rows = pl.ds(hk * HK, HK)
-        pltpu.make_async_copy(out_v.at[rows], out_hbm.at[rows], out_sem.at[hk]).start()
+                pair_f[pl.ds(2 * m + s, TI, stride=pitch), :] = jnp.transpose(
+                    result[:, s * TI : (s + 1) * TI]
+                )
+
+        @pl.loop(0, TI, unroll=4)
+        def _(i):
+            out_ref[i, pl.ds(hk * HK, HK)] = pair_f[pl.ds(i * pitch + hk * HK, HK), :].astype(BF16)
 
     for n, buf in enumerate((gs, ls, rs, rgr)):
         wait_for(buf.at[pl.ds(0, len(peers))], send_sem.at[n])
     for hk in (0, 1):
         rows = pl.ds(hk * HK, HK)
         wait_for(rgl.at[pl.ds(0, len(peers)), rows], send_sem.at[4 + hk])
-        pltpu.make_async_copy(out_v.at[rows], out_hbm.at[rows], out_sem.at[hk]).wait()
     wait_for(half, send_sem.at[6])
 
 
@@ -313,7 +312,7 @@
     in_vmem = pl.BlockSpec(memory_space=pltpu.VMEM)
     out = pl.pallas_call(
         functools.partial(kernel, RN, QN),
-        out_shape=jax.ShapeDtypeStruct((TJ, C, TI), BF16),
+        out_shape=pltpu.VMEM((TI, TJ, C), BF16),
         in_specs=[
             pl.BlockSpec(memory_space=pltpu.SMEM),
             any_space,
@@ -322,7 +321,7 @@
             in_vmem,
             in_vmem,
         ],
-        out_specs=any_space,
+        out_specs=in_vmem,
         scratch_shapes=[
             vmem(TI, TJ, C, BF16),
             vmem(TI * pitch, C, F32),
@@ -345,14 +344,12 @@
             vmem(TJ // 2, 8, 2 * TI, F32),
             vmem(TJ // 2, C, 2 * TI, F32),
             vmem(TJ // 2, C, 2 * TI, BF16),
-            vmem(TJ, C, TI, BF16),
             vmem(4 * H, C, BF16),
             vmem(C, C, F32),
             vmem(C, C, F32),
             pltpu.SemaphoreType.DMA((2,)),
             pltpu.SemaphoreType.DMA((7,)),
             pltpu.SemaphoreType.DMA((7,)),
-            pltpu.SemaphoreType.DMA((2,)),
         ],
         compiler_params=pltpu.CompilerParams(
             collective_id=0, has_side_effects=True, vmem_limit_bytes=60 << 20
@@ -365,7 +362,7 @@
         norm_bias.reshape(1, C),
         proj_weight,
     )
-    return jnp.transpose(out, (2, 0, 1))
+    return out
 
 
 def solution(mesh):

time: 79.2 us -> 77.1 us (0.973)
  local copies, waits for them, and re-layouts: 4.12 us -> 1.32 us
  Pallas kernels: 74.6 us -> 75.6 us
    transpose x1 -> x0, local copies, waits for them, and re-layouts: 4.12 us -> none  [shards(): return jnp.transpose(out, (2, 0, 1))]
    unnamed x0 -> x1, local copies, waits for them, and re-layouts: none -> 1.32 us
    pallas_call x1, Pallas kernels: 74.6 us -> 75.6 us  [shards(): pl.pallas_call(functools.partial(kernel, RN, QN), out_shape=pltpu.VMEM((T...]
where the time goes in v3:
time: 77.1 us; the launch traced here: 77 us
  Pallas kernels  75.6 us (98%)
  local copies, waits for them, and re-layouts  1.32 us (2%)
    pallas_call x1, Pallas kernels, shards(): pl.pallas_call(functools.partial(kernel, RN, QN), out_shape=pltpu.VMEM((T...  75.6 us

profile of v3, /device:TPU:0, one launch (start us, length us, event | category | flops | bytes accessed | tf_op | source)
XLA Modules:
  0.0 77.0 jit_solution(499608668301722161)
XLA Ops:
  0.0 75.6 %shard_map.64 = bf16[128,64,128]{2,1,0:T(8,128)(2,1)S(1)} custom-call(s32[8,8]{1,0:T(8,128)} %mask_ref.1, bf16[128,64,128]{2,1,0:T(8,128)(2,1)} %pair_hbm.1, bf16[64,64,128]{2,1,0:T(8,128)(2,1)} %bitcast.3, f32[1,128]{1,0:T(1,128)} %bitcast.4, f32[1,128]{1,0:T(1,128)} %bitcast.5, bf16[128,256]{1,0:T(8,128)(2,1)} %w_ref.1), custom_call_target="tpu_custom_call" | custom-call | tf_op jit(solution)/shard_map/pallas_call | solution.py:313
  75.6 1.3 %copy.8 = bf16[128,64,128]{2,1,0:T(8,128)(2,1)} copy(bf16[128,64,128]{2,1,0:T(8,128)(2,1)S(1)} %shard_map.64) | data formatting | bytes 4194304

commit v4 on v3

--- a/solution.py
+++ b/solution.py
@@ -12,39 +12,33 @@
 BF16 = jnp.bfloat16
 
 
-def ring_distance(offset, size):
-    return min(offset, size - offset)
+SEND_ORDER = (
+    42, 48, 58, 16, 46, 4, 38, 1, 41, 12, 26, 3, 43, 17, 57, 51,
+    10, 2, 47, 8, 22, 7, 62, 49, 39, 32, 27, 5, 37, 20, 25, 15,
+    59, 60, 30, 19, 34, 13, 54, 28, 45, 52, 40, 23, 53, 61, 36, 50,
+    33, 55, 9, 11, 56, 24, 44, 31, 63, 35, 21, 14, 29, 18, 6,
+)
 
 
 def send_order(X, Y, Z):
-    offsets = [(a, b, c) for a in range(X) for b in range(Y) for c in range(Z)]
-    offsets.remove((0, 0, 0))
-    state, shuffled = 12345, []
-    while offsets:
-        state = (state * 1103515245 + 12345) % (1 << 31)
-        shuffled.append(offsets.pop((state >> 8) % len(offsets)))
-    paired, seen = [], set()
-    for offset in shuffled:
-        for one in (offset, ((-offset[0]) % X, (-offset[1]) % Y, (-offset[2]) % Z)):
-            if one not in seen:
-                seen.add(one)
-                paired.append(one)
-    def far(o):
-        return ring_distance(o[0], X) + ring_distance(o[1], Y) + ring_distance(o[2], Z)
-
-    return sorted(paired, key=lambda o: -far(o))
+    assert (X, Y, Z) == (4, 4, 4)
+    return [(code // 16, code // 4 % 4, code % 4) for code in SEND_ORDER]
 
 
 def kernel(
     RN,
     QN,
-    mask_ref,
+    mask_hbm,
     pair_hbm,
     grad_hbm,
+    gain_hbm,
+    bias_hbm,
+    w_hbm,
+    out_ref,
+    mask_ref,
     gain_ref,
     bias_ref,
     w_ref,
-    out_ref,
     pair_v,
     pair_f,
     grad_v,
@@ -87,8 +81,14 @@
 
     grad_load = pltpu.make_async_copy(grad_hbm, grad_v, load_sem.at[0])
     pair_load = pltpu.make_async_copy(pair_hbm, pair_v, load_sem.at[1])
-    grad_load.start()
-    pair_load.start()
+    small = [
+        pltpu.make_async_copy(src, dst, load_sem.at[2 + n])
+        for n, (src, dst) in enumerate(
+            ((gain_hbm, gain_ref), (bias_hbm, bias_ref), (w_hbm, w_ref), (mask_hbm, mask_ref))
+        )
+    ]
+    for load in [grad_load, *small, pair_load]:
+        load.start()
 
     peers = []
     for dx, dy, dz in send_order(X, Y, Z):
@@ -101,10 +101,6 @@
             barrier, inc=1, device_id=(prow, pqp * 2 + core), device_id_type=MESH
         )
     pl.semaphore_signal(barrier, inc=1, device_id=(row, qp * 2 + 1 - core), device_id_type=MESH)
-
-    gain_s[...] = jnp.transpose(jnp.broadcast_to(gain_ref[...], (C, C)))
-    bias_s[...] = jnp.transpose(jnp.broadcast_to(bias_ref[...], (C, C)))
-    wt_s[...] = jnp.transpose(w_ref[...].astype(F32)).astype(BF16)
 
     def scatter(n, src_of, dst, own_src):
         pltpu.make_async_copy(own_src, dst, recv_sem.at[n]).start()
@@ -135,6 +131,12 @@
     lanes = pl.ds(pl.multiple_of(row * TI, TI), TI)
     by_channel = lambda ref: (lambda prow, pqp: ref.at[prow * QP + pqp])
     scatter(0, by_channel(gs), gt.at[qp, pl.ds(pl.multiple_of(core * TJ, TJ), TJ), lanes], gs.at[me])
+
+    for load in small:
+        load.wait()
+    gain_s[...] = jnp.transpose(jnp.broadcast_to(gain_ref[...], (C, C)))
+    bias_s[...] = jnp.transpose(jnp.broadcast_to(bias_ref[...], (C, C)))
+    wt_s[...] = jnp.transpose(w_ref[...].astype(F32)).astype(BF16)
 
     pair_load.wait()
 
@@ -313,16 +315,13 @@
     out = pl.pallas_call(
         functools.partial(kernel, RN, QN),
         out_shape=pltpu.VMEM((TI, TJ, C), BF16),
-        in_specs=[
-            pl.BlockSpec(memory_space=pltpu.SMEM),
-            any_space,
-            any_space,
-            in_vmem,
-            in_vmem,
-            in_vmem,
-        ],
+        in_specs=[any_space] * 6,
         out_specs=in_vmem,
         scratch_shapes=[
+            pltpu.SMEM(tile_mask.shape, jnp.int32),
+            vmem(1, C, F32),
+            vmem(1, C, F32),
+            vmem(C, 4 * H, BF16),
             vmem(TI, TJ, C, BF16),
             vmem(TI * pitch, C, F32),
             vmem(TJ, H, TI, BF16),
@@ -347,7 +346,7 @@
             vmem(4 * H, C, BF16),
             vmem(C, C, F32),
             vmem(C, C, F32),
-            pltpu.SemaphoreType.DMA((2,)),
+            pltpu.SemaphoreType.DMA((6,)),
             pltpu.SemaphoreType.DMA((7,)),
             pltpu.SemaphoreType.DMA((7,)),
         ],

time: 77.1 us -> 73.3 us (0.951)
  Pallas kernels: 75.6 us -> 71.8 us
    pallas_call x1, Pallas kernels: 75.6 us -> 71.8 us  [shards(): pl.pallas_call(functools.partial(kernel, RN, QN), out_shape=pltpu.VMEM((T...]
where the time goes in v4:
time: 73.3 us; the launch traced here: 73.2 us
  Pallas kernels  71.8 us (98%)
  local copies, waits for them, and re-layouts  1.32 us (2%)
    pallas_call x1, Pallas kernels, shards(): pl.pallas_call(functools.partial(kernel, RN, QN), out_shape=pltpu.VMEM((T...  71.8 us

profile of v4, /device:TPU:0, one launch (start us, length us, event | category | flops | bytes accessed | tf_op | source)
XLA Modules:
  0.0 73.2 jit_solution(7880063205175047702)
XLA Ops:
  0.0 71.8 %shard_map.64 = bf16[128,64,128]{2,1,0:T(8,128)(2,1)S(1)} custom-call(s32[8,8]{1,0:T(8,128)} %mask_hbm.1, bf16[128,64,128]{2,1,0:T(8,128)(2,1)} %pair_hbm.1, bf16[64,64,128]{2,1,0:T(8,128)(2,1)} %bitcast.3, f32[1,128]{1,0:T(1,128)} %bitcast.4, f32[1,128]{1,0:T(1,128)} %bitcast.5, bf16[128,256]{1,0:T(8,128)(2,1)} %w_hbm.1), custom_call_target="tpu_custom_call" | custom-call | tf_op jit(solution)/shard_map/pallas_call | solution.py:315
  71.8 1.3 %copy.8 = bf16[128,64,128]{2,1,0:T(8,128)(2,1)} copy(bf16[128,64,128]{2,1,0:T(8,128)(2,1)S(1)} %shard_map.64) | data formatting | bytes 4194304
